TPU v7x, 256 devices: a whole 4x4x8 slice. The times are simulated.
256 devices in a mesh: ctx: 16 (over y_hi, x, core), dp: 16 (over y_lo, z).
Axes of the slice: x: 4, y: 4 (y_hi: 2, y_lo: 2; y = y_hi * 2 + y_lo), z: 8, core: 2. Of those that a mesh axis runs over, the one named last changes fastest.
Arguments:
- queries: bfloat16 [16, 2048, 1536], P('dp', 'ctx'), as said below
- keys: bfloat16 [16, 2048, 1536], P('dp', 'ctx'), as said below
- values: bfloat16 [16, 2048, 1536], P('dp', 'ctx'), may hold values from -6 to 6
- tangent_queries: bfloat16 [16, 2048, 1536], P('dp', 'ctx'), may hold values from -6 to 6
- tangent_keys: bfloat16 [16, 2048, 1536], P('dp', 'ctx'), may hold values from -6 to 6
- tangent_values: bfloat16 [16, 2048, 1536], P('dp', 'ctx'), may hold values from -6 to 6
- clip_ids: int32 [16, 2048], P('dp', 'ctx'), may hold values from 0 to 3, never falling along the last dimension, each value on 1 to 1024 neighbouring positions
- block_order: int32 [16], replicated, may hold values from 0 to 15, each once
- out_weight: bfloat16 [1536, 3072], replicated, may hold values from -0.15625 to 0.15625
- layer_scale: float32 [3072], replicated, may hold values from 0.1 to 1.9
- cotangent: bfloat16 [16, 2048, 3072], P('dp', 'ctx'), as said below
Outputs:
- tangent_branch: bfloat16 [16, 2048, 3072], P('dp', 'ctx')
- scale_grad: float32 [3072], replicated
Inputs may be any that keep to these rules, and one draw needn't show every extreme that they name: `clip_ids`: ids never fall along a sample's rows; each of the 4 clips is a run of consecutive rows. `block_order`: each block number appears once. `queries`: real-valued. `keys`: real-valued. `cotangent`: real-valued.
All inputs are finite; a program needn't handle non-finite values.
Results may differ from a plain program's by a relative error of at most 0.02.
The roundings to bfloat16 on the way count: a program that leaves them out, or rounds other values in their place, can miss the bound.
Values may be sent and summed in bfloat16 or wider, within the bound.
A program may use at most 192 MiB of HBM per device.

v0:
```python
import math
import jax
import jax.numpy as jnp
from jax import lax
from jax.sharding import PartitionSpec as P

HEADS = 12


def rotate(x, pos, half_dim):
    frequency = 10000.0 ** (-jnp.arange(half_dim, dtype=jnp.float32) / half_dim)
    angles = pos.astype(jnp.float32)[:, None] * frequency[None, :]
    cosine = jnp.cos(angles)[:, None, :]
    sine_part = jnp.sin(angles)[:, None, :]
    front_part = x[..., :half_dim]
    back_part = x[..., half_dim:]
    return jnp.concatenate(
        [front_part * cosine - back_part * sine_part, back_part * cosine + front_part * sine_part],
        axis=-1,
    )


def make_attend(query_rot, tquery_rot, query_ids, scale):

    def attend(carry, block):
        best, total, weighted, primal_acc, slope_acc, spread_acc = carry
        key_blk, value_blk, tkey_blk, tvalue_blk, key_ids = block
        scores = (
            jnp.einsum("hqd,hkd->hqk", query_rot, key_blk, preferred_element_type=jnp.float32)
            * scale
        )
        same_clip = query_ids[:, None] == key_ids[None, :]
        scores = jnp.where(same_clip[None], scores, -jnp.inf)
        slopes = (
            jnp.einsum("hqd,hkd->hqk", tquery_rot, key_blk, preferred_element_type=jnp.float32)
            + jnp.einsum("hqd,hkd->hqk", query_rot, tkey_blk, preferred_element_type=jnp.float32)
        ) * scale
        new_best = jnp.maximum(best, jnp.max(scores, axis=-1))
        factor = jnp.exp(best - new_best)
        weights = jnp.exp(scores - new_best[..., None])
        tilted = weights * slopes
        total = total * factor + jnp.sum(weights, axis=-1)
        weighted = weighted * factor + jnp.sum(tilted, axis=-1)
        weights_b = weights.astype(jnp.bfloat16)
        tilted_b = tilted.astype(jnp.bfloat16)
        primal_acc = primal_acc * factor[..., None] + jnp.einsum(
            "hqk,hkd->hqd", weights_b, value_blk, preferred_element_type=jnp.float32
        )
        slope_acc = slope_acc * factor[..., None] + jnp.einsum(
            "hqk,hkd->hqd", tilted_b, value_blk, preferred_element_type=jnp.float32
        )
        spread_acc = spread_acc * factor[..., None] + jnp.einsum(
            "hqk,hkd->hqd", weights_b, tvalue_blk, preferred_element_type=jnp.float32
        )
        return ((new_best, total, weighted, primal_acc, slope_acc, spread_acc), None)

    return attend


def start_states(heads, rows, head_dim):
    zeros_rows = jnp.zeros((heads, rows), jnp.float32)
    zeros_heads = jnp.zeros((heads, rows, head_dim), jnp.float32)
    return (
        jnp.full((heads, rows), -1e30, jnp.float32),
        zeros_rows,
        zeros_rows,
        zeros_heads,
        zeros_heads,
        zeros_heads,
    )


def local(
    queries,
    keys,
    values,
    tangent_queries,
    tangent_keys,
    tangent_values,
    clip_ids,
    block_order,
    out_weight,
    layer_scale,
    cotangent,
):
    tok_rows = queries.shape[1]
    heads = HEADS
    head_dim = queries.shape[2] // heads
    scale = head_dim ** (-0.5)
    cycle_index = lax.axis_index("ctx")
    positions = block_order[cycle_index] * tok_rows + jnp.arange(tok_rows, dtype=jnp.int32)

    def heads_first(x, turned):
        y = x[0].reshape(tok_rows, heads, head_dim)
        if turned:
            y = rotate(y.astype(jnp.float32), positions, head_dim // 2).astype(jnp.bfloat16)
        return jnp.transpose(y, (1, 0, 2))

    query_rot = heads_first(queries, True)
    key_rot = heads_first(keys, True)
    value_heads = heads_first(values, False)
    tquery_rot = heads_first(tangent_queries, True)
    tkey_rot = heads_first(tangent_keys, True)
    tvalue_heads = heads_first(tangent_values, False)
    all_ids = lax.all_gather(clip_ids, "ctx", axis=1, tiled=True)[0]
    own_ids = clip_ids[0]
    attend = make_attend(query_rot, tquery_rot, own_ids, scale)
    carry = start_states(heads, tok_rows, head_dim)
    key_part = lax.all_gather(key_rot, "ctx", axis=1, tiled=True)
    value_part = lax.all_gather(value_heads, "ctx", axis=1, tiled=True)
    tkey_part = lax.all_gather(tkey_rot, "ctx", axis=1, tiled=True)
    tvalue_part = lax.all_gather(tvalue_heads, "ctx", axis=1, tiled=True)
    count = key_part.shape[1]
    block_rows = math.gcd(count, tok_rows)
    blocks = count // block_rows

    def split_blocks(x):
        return jnp.transpose(x.reshape(heads, blocks, block_rows, head_dim), (1, 0, 2, 3))

    stacked = (
        split_blocks(key_part),
        split_blocks(value_part),
        split_blocks(tkey_part),
        split_blocks(tvalue_part),
        all_ids.reshape(blocks, block_rows),
    )
    carry, unused = lax.scan(attend, carry, stacked)
    best, total, weighted, primal_acc, slope_acc, spread_acc = carry
    mean_out = primal_acc / total[..., None]
    tangent_heads = (
        (slope_acc + spread_acc) / total[..., None] - (weighted / total)[..., None] * mean_out
    ).astype(jnp.bfloat16)
    tangent_rows = jnp.transpose(tangent_heads, (1, 0, 2)).reshape(tok_rows, heads * head_dim)
    projected = jnp.dot(tangent_rows, out_weight, preferred_element_type=jnp.float32)
    branch = (layer_scale * projected).astype(jnp.bfloat16)[None]
    partial_grad = jnp.sum(cotangent[0].astype(jnp.float32) * projected, axis=0)
    summed = lax.psum(partial_grad, ("ctx", "dp"))
    count_all = lax.axis_size("ctx") * lax.axis_size("dp") * tok_rows
    return (branch, summed / math.sqrt(count_all))


def solution(mesh):
    in_specs = (
        P("dp", "ctx", None),
        P("dp", "ctx", None),
        P("dp", "ctx", None),
        P("dp", "ctx", None),
        P("dp", "ctx", None),
        P("dp", "ctx", None),
        P("dp", "ctx"),
        P(),
        P(),
        P(),
        P("dp", "ctx", None),
    )
    out_specs = (P("dp", "ctx", None), P())
    return jax.shard_map(local, mesh=mesh, in_specs=in_specs, out_specs=out_specs, check_vma=False)
```

profile of v0, /device:TPU:1, one launch (start us, length us, event | category | flops | bytes accessed | tf_op | source)
XLA Modules:
  0.0 623.5 jit_solution(16415383374081786712)
XLA Ops:
  18.6 1.9 copy.28
  22.8 25.8 %all_gather.15 = s32[1,2048]{1,0:T(1,128)} all-gather(s32[1,128]{1,0:T(1,128)} %param.19), channel_id=1, replica_groups=mesh['ctx'=16,'dp'=16] {'ctx'}, dimensions={1}, use_global_device_ids=true | all-gather | bytes 8704 | tf_op jit(solution)/shard_map/all_gather | solution.py:105
  48.7 46.9 %all-gather.5.cloned.1.call-done = bf16[12,2048,128]{1,2,0:T(8,128)(2,1)} async-done(((bf16[12,128,128]{1,2,0:T(8,128)(2,1)}), bf16[12,2048,128]{1,2,0:T(8,128)(2,1)}) %all-gather.5.cloned.1.call-update) | async-done | bytes 6291472 | tf_op jit(solution)/shard_map/all_gather | solution.py:109
  95.6 7.8 %copy.44 = bf16[192,8,16,128]{3,2,1,0:T(8,128)(2,1)} copy(bf16[192,8,16,128]{3,1,2,0:T(8,128)(2,1)} %bitcast.120) | data formatting | bytes 12582912
  103.3 9.0 %copy.21 = bf16[12,16,128,128]{3,2,0,1:T(8,128)(2,1)} copy(bf16[12,16,128,128]{2,1,3,0:T(8,128)(2,1)} %bitcast.115) | data formatting | bytes 12582912 | tf_op jit(solution)/shard_map/reshape | solution.py:118
  112.4 58.9 %all-gather.7.cloned.1.call-done = bf16[12,2048,128]{1,2,0:T(8,128)(2,1)} async-done(((bf16[12,128,128]{1,2,0:T(8,128)(2,1)}), bf16[12,2048,128]{1,2,0:T(8,128)(2,1)}) %all-gather.7.cloned.1.call-update) | async-done | bytes 6291472 | tf_op jit(solution)/shard_map/all_gather | solution.py:111
  171.3 8.7 %copy.25 = bf16[12,2048,128]{2,1,0:T(8,128)(2,1)} copy(bf16[12,2048,128]{1,2,0:T(8,128)(2,1)} %all-gather.7.cloned.1.call-done) | data formatting | bytes 12582912 | tf_op jit(solution)/shard_map/all_gather | solution.py:111
  180.0 67.1 %all-gather.9.cloned.1.call-done = bf16[12,2048,128]{1,2,0:T(8,128)(2,1)} async-done(((bf16[12,128,128]{1,2,0:T(8,128)(2,1)}), bf16[12,2048,128]{1,2,0:T(8,128)(2,1)}) %all-gather.9.cloned.1.call-update) | async-done | bytes 6291472 | tf_op jit(solution)/shard_map/all_gather | solution.py:110
  247.1 8.6 %copy.27 = bf16[12,2048,128]{2,1,0:T(8,128)(2,1)} copy(bf16[12,2048,128]{1,2,0:T(8,128)(2,1)} %all-gather.9.cloned.1.call-done) | data formatting | bytes 12582912 | tf_op jit(solution)/shard_map/all_gather | solution.py:110
  255.7 67.0 %all-gather.11.cloned.1.call-done = bf16[12,2048,128]{1,2,0:T(8,128)(2,1)} async-done(((bf16[12,128,128]{1,2,0:T(8,128)(2,1)}), bf16[12,2048,128]{1,2,0:T(8,128)(2,1)}) %all-gather.11.cloned.1.call-update) | async-done | bytes 6291472 | tf_op jit(solution)/shard_map/all_gather | solution.py:112
  322.7 8.7 %copy.29 = bf16[12,2048,128]{2,1,0:T(8,128)(2,1)} copy(bf16[12,2048,128]{1,2,0:T(8,128)(2,1)} %all-gather.11.cloned.1.call-done) | data formatting | bytes 12582912 | tf_op jit(solution)/shard_map/all_gather | solution.py:112
  331.3 200.5 %while.21 = (s32[]{:T(128)}, f32[12,128]{1,0:T(8,128)S(1)}, f32[12,128]{1,0:T(8,128)}, f32[12,128]{1,0:T(8,128)}, f32[12,128,128]{2,1,0:T(8,128)S(1)}, /*index=5...) while((s32[]{:T(128)}, f32[12,128]{1,0:T(8,128)S(1)}, ...), condition=%wide.region_4.5_spmd.clone, body=%wide.region_0.4_spmd.clone.sunk | while | flops 306735616 | bytes 14789864 | solution.py:127
  340.9 1.6 convolution_add_fusion.7
  351.9 1.6 convolution_add_fusion.8
  353.5 1.6 convolution_add_fusion.7
  366.0 1.6 convolution_add_fusion.7
  377.0 1.6 convolution_add_fusion.8
  378.6 1.6 convolution_add_fusion.7
  391.2 1.6 convolution_add_fusion.7
  403.8 1.6 convolution_add_fusion.7
  416.3 1.6 convolution_add_fusion.7
  428.9 1.6 convolution_add_fusion.7
  441.5 1.6 convolution_add_fusion.7
  454.1 1.6 convolution_add_fusion.7
  466.6 1.6 convolution_add_fusion.7
  479.2 1.6 convolution_add_fusion.7
  491.8 1.6 convolution_add_fusion.7
  504.3 1.6 convolution_add_fusion.7
  516.9 1.6 convolution_add_fusion.7
  529.5 1.6 convolution_add_fusion.7
  534.3 6.4 %fusion.32 = (f32[3072]{0:T(1024)S(1)}, bf16[1,128,3072]{2,1,0:T(8,128)(2,1)}) fusion(bf16[1,128,3072]{2,1,0:T(8,128)(2,1)} %param.23, f32[3072]{0:T(1024)S(1)} %copy-done.3, bf16[128,1536]{0,1:T(8,128)(2,1)S(1)} %bitcast.121, bf16[1536,3072]{1,0:T(8,128)(2,1)} %param.21), kind=kOutput, calls=%fused_computation.46 | convolution fusion | flops 1209922560 | bytes 11427840 | tf_op jit(solution)/shard_map/dot_general | solution.py:134
  540.7 75.7 %psum.7 = f32[3072]{0:T(1024)S(1)} all-reduce(f32[3072]{0:T(1024)S(1)} %get-tuple-element.187), channel_id=1, replica_groups=mesh['ctx'=16,'dp'=16] {'ctx','dp'}, use_global_device_ids=true, to_apply=%region_6.7 | all-reduce | flops 3072 | bytes 24576 | tf_op jit(solution)/shard_map/psum | solution.py:137
  (297 shorter events, 186.4 us)
Async XLA Ops:
  7.2 88.4 %all-gather.5.cloned.1.call-start = ((), (), s32[]{:S(2)}) async-start(), calls=%async_computation | async-start | bytes 6684672 | tf_op jit(solution)/shard_map/all_gather | solution.py:109
  11.7 5.9 copy-start.2
  16.6 154.7 %all-gather.7.cloned.1.call-start = ((), (), s32[]{:S(2)}) async-start(), calls=%async_computation.1 | async-start | bytes 6684672 | tf_op jit(solution)/shard_map/all_gather | solution.py:111
  17.5 229.6 %all-gather.9.cloned.1.call-start = ((), (), s32[]{:S(2)}) async-start(), calls=%async_computation.2 | async-start | bytes 6684672 | tf_op jit(solution)/shard_map/all_gather | solution.py:110
  18.5 304.1 %all-gather.11.cloned.1.call-start = ((), (), s32[]{:S(2)}) async-start(), calls=%async_computation.3 | async-start | bytes 6684672 | tf_op jit(solution)/shard_map/all_gather | solution.py:112
  334.2 8.4 %copy-start = (f32[12,128]{1,0:T(8,128)S(1)}, f32[12,128]{1,0:T(8,128)}, u32[]{:S(2)}) copy-start(f32[12,128]{1,0:T(8,128)} %get-tuple-element.331) | copy-start | bytes 18436 | tf_op jit(solution)/shard_map/while
  346.1 9.1 %copy-start = (f32[12,128]{1,0:T(8,128)S(1)}, f32[12,128]{1,0:T(8,128)}, u32[]{:S(2)}) copy-start(f32[12,128]{1,0:T(8,128)} %get-tuple-element.331) | copy-start | bytes 18436 | tf_op jit(solution)/shard_map/while
  355.2 0.6 copy-start.1
  358.6 9.1 %copy-start = (f32[12,128]{1,0:T(8,128)S(1)}, f32[12,128]{1,0:T(8,128)}, u32[]{:S(2)}) copy-start(f32[12,128]{1,0:T(8,128)} %get-tuple-element.331) | copy-start | bytes 18436 | tf_op jit(solution)/shard_map/while
  367.8 0.6 copy-start.1
  371.2 9.1 %copy-start = (f32[12,128]{1,0:T(8,128)S(1)}, f32[12,128]{1,0:T(8,128)}, u32[]{:S(2)}) copy-start(f32[12,128]{1,0:T(8,128)} %get-tuple-element.331) | copy-start | bytes 18436 | tf_op jit(solution)/shard_map/while
  383.8 9.1 %copy-start = (f32[12,128]{1,0:T(8,128)S(1)}, f32[12,128]{1,0:T(8,128)}, u32[]{:S(2)}) copy-start(f32[12,128]{1,0:T(8,128)} %get-tuple-element.331) | copy-start | bytes 18436 | tf_op jit(solution)/shard_map/while
  392.9 0.6 copy-start.1
  396.4 9.1 %copy-start = (f32[12,128]{1,0:T(8,128)S(1)}, f32[12,128]{1,0:T(8,128)}, u32[]{:S(2)}) copy-start(f32[12,128]{1,0:T(8,128)} %get-tuple-element.331) | copy-start | bytes 18436 | tf_op jit(solution)/shard_map/while
  405.5 0.6 copy-start.1
  408.9 9.1 %copy-start = (f32[12,128]{1,0:T(8,128)S(1)}, f32[12,128]{1,0:T(8,128)}, u32[]{:S(2)}) copy-start(f32[12,128]{1,0:T(8,128)} %get-tuple-element.331) | copy-start | bytes 18436 | tf_op jit(solution)/shard_map/while
  418.1 0.6 copy-start.1
  421.5 9.1 %copy-start = (f32[12,128]{1,0:T(8,128)S(1)}, f32[12,128]{1,0:T(8,128)}, u32[]{:S(2)}) copy-start(f32[12,128]{1,0:T(8,128)} %get-tuple-element.331) | copy-start | bytes 18436 | tf_op jit(solution)/shard_map/while
  430.6 0.6 copy-start.1
  434.1 9.1 %copy-start = (f32[12,128]{1,0:T(8,128)S(1)}, f32[12,128]{1,0:T(8,128)}, u32[]{:S(2)}) copy-start(f32[12,128]{1,0:T(8,128)} %get-tuple-element.331) | copy-start | bytes 18436 | tf_op jit(solution)/shard_map/while
  443.2 0.6 copy-start.1
  446.7 9.1 %copy-start = (f32[12,128]{1,0:T(8,128)S(1)}, f32[12,128]{1,0:T(8,128)}, u32[]{:S(2)}) copy-start(f32[12,128]{1,0:T(8,128)} %get-tuple-element.331) | copy-start | bytes 18436 | tf_op jit(solution)/shard_map/while
  455.8 0.6 copy-start.1
  459.2 9.1 %copy-start = (f32[12,128]{1,0:T(8,128)S(1)}, f32[12,128]{1,0:T(8,128)}, u32[]{:S(2)}) copy-start(f32[12,128]{1,0:T(8,128)} %get-tuple-element.331) | copy-start | bytes 18436 | tf_op jit(solution)/shard_map/while
  471.8 9.1 %copy-start = (f32[12,128]{1,0:T(8,128)S(1)}, f32[12,128]{1,0:T(8,128)}, u32[]{:S(2)}) copy-start(f32[12,128]{1,0:T(8,128)} %get-tuple-element.331) | copy-start | bytes 18436 | tf_op jit(solution)/shard_map/while
  480.9 0.6 copy-start.1
  484.4 9.1 %copy-start = (f32[12,128]{1,0:T(8,128)S(1)}, f32[12,128]{1,0:T(8,128)}, u32[]{:S(2)}) copy-start(f32[12,128]{1,0:T(8,128)} %get-tuple-element.331) | copy-start | bytes 18436 | tf_op jit(solution)/shard_map/while
  496.9 9.1 %copy-start = (f32[12,128]{1,0:T(8,128)S(1)}, f32[12,128]{1,0:T(8,128)}, u32[]{:S(2)}) copy-start(f32[12,128]{1,0:T(8,128)} %get-tuple-element.331) | copy-start | bytes 18436 | tf_op jit(solution)/shard_map/while
  506.1 0.6 copy-start.1
  509.5 9.1 %copy-start = (f32[12,128]{1,0:T(8,128)S(1)}, f32[12,128]{1,0:T(8,128)}, u32[]{:S(2)}) copy-start(f32[12,128]{1,0:T(8,128)} %get-tuple-element.331) | copy-start | bytes 18436 | tf_op jit(solution)/shard_map/while
  522.1 9.1 %copy-start = (f32[12,128]{1,0:T(8,128)S(1)}, f32[12,128]{1,0:T(8,128)}, u32[]{:S(2)}) copy-start(f32[12,128]{1,0:T(8,128)} %get-tuple-element.331) | copy-start | bytes 18436 | tf_op jit(solution)/shard_map/while
  531.8 2.5 copy-start.3
  (6 other events, 3.6 us)
Sparse Core Ops, SparseCore 0:
  16.7 78.7 all-gather.4
  98.1 73.1 all-gather.6
  173.9 73.1 all-gather.8
  249.5 73.1 all-gather.10
where the time goes:
time: 630 us; the launch traced here: 623 us
  waiting for transfers between devices  240 us (38%)
  matrix products  150 us (24%)
  blocking collectives  102 us (16%)
  local copies, waits for them, and re-layouts  74 us (12%)
  other arithmetic  41 us (7%)
  between operations  14.6 us (2%)
    psum x1, blocking collectives, local(): summed = lax.psum(partial_grad, ('ctx', 'dp'))  75.7 us
    all_gather x1, waiting for transfers between devices, local(): value_part = lax.all_gather(value_heads, 'ctx', axis=1, tiled=True)  67.1 us
    all_gather x1, waiting for transfers between devices, local(): tvalue_part = lax.all_gather(tvalue_heads, 'ctx', axis=1, tiled=True)  67 us
    all_gather x1, waiting for transfers between devices, local(): tkey_part = lax.all_gather(tkey_rot, 'ctx', axis=1, tiled=True)  58.9 us
    all_gather x1, waiting for transfers between devices, local(): key_part = lax.all_gather(key_rot, 'ctx', axis=1, tiled=True)  46.9 us
    all_gather x1, blocking collectives, local(): all_ids = lax.all_gather(clip_ids, 'ctx', axis=1, tiled=True)[0]  25.8 us
    dot_general x16, matrix products, attend(): jnp.einsum('hqk,hkd->hqd', weights_b, value_blk, preferred_element_type=j...  25.1 us
    dot_general x16, matrix products, attend(): jnp.einsum('hqk,hkd->hqd', tilted_b, value_blk, preferred_element_type=jn...  24.9 us
  transfers between devices with their start and end apart: 4, of which 4 were waited for; matrix products, arithmetic and copies ran while one was open for 6% of the time, Pallas kernels for 0%

commit v1 on v0

--- a/solution.py
+++ b/solution.py
@@ -109,7 +109,17 @@
     key_part = lax.all_gather(key_rot, "ctx", axis=1, tiled=True)
     value_part = lax.all_gather(value_heads, "ctx", axis=1, tiled=True)
     tkey_part = lax.all_gather(tkey_rot, "ctx", axis=1, tiled=True)
-    tvalue_part = lax.all_gather(tvalue_heads, "ctx", axis=1, tiled=True)
+
+    def _balance_table(frame_in):
+        z_new = lax.all_to_all(
+            jnp.stack([frame_in for _ in range(lax.axis_size("ctx"))], axis=0),
+            concat_axis=0,
+            axis_name="ctx",
+            split_axis=0,
+        )
+        return jnp.concatenate(z_new, 1)
+
+    tvalue_part = _balance_table(tvalue_heads)
     count = key_part.shape[1]
     block_rows = math.gcd(count, tok_rows)
     blocks = count // block_rows

time: 630 us -> 604 us (0.959)
  waiting for transfers between devices: 240 us -> 138 us
  blocking collectives: 102 us -> 174 us
  starting transfers between devices: 0.16 us -> 8.57 us
    all_gather x1, blocking collectives: 25.8 us -> 98.7 us  [local(): all_ids = lax.all_gather(clip_ids, 'ctx', axis=1, tiled=True)[0]]
    all_gather x1 -> x0, waiting for transfers between devices: 67 us -> none  [local(): tvalue_part = lax.all_gather(tvalue_heads, 'ctx', axis=1, tiled=True)]
    all_gather x1, waiting for transfers between devices: 46.9 us -> 13 us  [local(): key_part = lax.all_gather(key_rot, 'ctx', axis=1, tiled=True)]
    all_gather x1 -> x0, local copies, waits for them, and re-layouts: 8.67 us -> none  [local(): tvalue_part = lax.all_gather(tvalue_heads, 'ctx', axis=1, tiled=True)]
    all_to_all x0 -> x1, starting transfers between devices: none -> 8.45 us  [_balance_table(): lax.all_to_all(jnp.stack([frame_in for _ in range(lax.axis_size('ctx'))],...]
  transfers between devices with their start and end apart: 4 -> 4, of which waited for: 4 -> 3; matrix products, arithmetic and copies ran while one was open for 6% -> 7% of each run, Pallas kernels for 0% -> 0%
where the time goes in v1:
time: 604 us; the launch traced here: 598 us
  blocking collectives  174 us (29%)
  matrix products  150 us (25%)
  waiting for transfers between devices  138 us (23%)
  local copies, waits for them, and re-layouts  69.3 us (11%)
  other arithmetic  41 us (7%)
  between operations  14.6 us (2%)
  starting transfers between devices  8.57 us (1%)
    all_gather x1, blocking collectives, local(): all_ids = lax.all_gather(clip_ids, 'ctx', axis=1, tiled=True)[0]  98.7 us
    psum x1, blocking collectives, local(): summed = lax.psum(partial_grad, ('ctx', 'dp'))  75.7 us
    all_gather x1, waiting for transfers between devices, local(): value_part = lax.all_gather(value_heads, 'ctx', axis=1, tiled=True)  67.2 us
    all_gather x1, waiting for transfers between devices, local(): tkey_part = lax.all_gather(tkey_rot, 'ctx', axis=1, tiled=True)  58.2 us
    dot_general x16, matrix products, attend(): jnp.einsum('hqk,hkd->hqd', weights_b, value_blk, preferred_element_type=j...  25.1 us
    dot_general x16, matrix products, attend(): jnp.einsum('hqk,hkd->hqd', tilted_b, value_blk, preferred_element_type=jn...  24.9 us
    dot_general x16, matrix products, attend(): jnp.einsum('hqk,hkd->hqd', weights_b, tvalue_blk, preferred_element_type=...  24.8 us
    dot_general x16, matrix products, attend(): jnp.einsum('hqd,hkd->hqk', tquery_rot, key_blk, preferred_element_type=jn...  24.1 us
  transfers between devices with their start and end apart: 4, of which 3 were waited for; matrix products, arithmetic and copies ran while one was open for 7% of the time, Pallas kernels for 0%

profile of v1, /device:TPU:1, one launch (start us, length us, event | category | flops | bytes accessed | tf_op | source)
XLA Modules:
  0.0 598.3 jit_solution(16564892859626204754)
XLA Ops:
  20.0 4.3 stack.2
  24.3 8.4 %all-to-all-start = ((bf16[16,12,128,128]{3,2,1,0:T(8,128)(2,1)}), bf16[16,12,128,128]{3,2,1,0:T(8,128)(2,1)}, u32[]{:S(2)}, u32[]{:S(2)}) async-start(bf16[16,12,128,128]{3,2,1,0:T(8,128)(2,1)} %stack.2), calls=%async_computation | async-start | bytes 12582912 | tf_op jit(solution)/shard_map/all_to_all | solution.py:114
  35.1 98.7 %all_gather.12 = s32[1,2048]{1,0:T(1,128)} all-gather(s32[1,128]{1,0:T(1,128)} %param.19), channel_id=1, replica_groups=mesh['ctx'=16,'dp'=16] {'ctx'}, dimensions={1}, use_global_device_ids=true | all-gather | bytes 8704 | tf_op jit(solution)/shard_map/all_gather | solution.py:105
  133.8 13.0 %all-gather.4.cloned.1.call-done = bf16[12,2048,128]{1,2,0:T(8,128)(2,1)} async-done(((bf16[12,128,128]{1,2,0:T(8,128)(2,1)}), bf16[12,2048,128]{1,2,0:T(8,128)(2,1)}) %all-gather.4.cloned.1.call-update) | async-done | bytes 6291472 | tf_op jit(solution)/shard_map/all_gather | solution.py:109
  146.8 7.7 %copy.43 = bf16[192,8,16,128]{3,2,1,0:T(8,128)(2,1)} copy(bf16[192,8,16,128]{3,1,2,0:T(8,128)(2,1)} %bitcast.114) | data formatting | bytes 12582912
  154.5 9.0 %copy.22 = bf16[12,16,128,128]{3,2,0,1:T(8,128)(2,1)} copy(bf16[12,16,128,128]{2,1,3,0:T(8,128)(2,1)} %bitcast.110) | data formatting | bytes 12582912 | tf_op jit(solution)/shard_map/reshape | solution.py:128
  163.5 58.2 %all-gather.6.cloned.1.call-done = bf16[12,2048,128]{1,2,0:T(8,128)(2,1)} async-done(((bf16[12,128,128]{1,2,0:T(8,128)(2,1)}), bf16[12,2048,128]{1,2,0:T(8,128)(2,1)}) %all-gather.6.cloned.1.call-update) | async-done | bytes 6291472 | tf_op jit(solution)/shard_map/all_gather | solution.py:111
  221.7 8.6 %copy.26 = bf16[12,2048,128]{2,1,0:T(8,128)(2,1)} copy(bf16[12,2048,128]{1,2,0:T(8,128)(2,1)} %all-gather.6.cloned.1.call-done) | data formatting | bytes 12582912 | tf_op jit(solution)/shard_map/all_gather | solution.py:111
  230.3 67.2 %all-gather.8.cloned.1.call-done = bf16[12,2048,128]{1,2,0:T(8,128)(2,1)} async-done(((bf16[12,128,128]{1,2,0:T(8,128)(2,1)}), bf16[12,2048,128]{1,2,0:T(8,128)(2,1)}) %all-gather.8.cloned.1.call-update) | async-done | bytes 6291472 | tf_op jit(solution)/shard_map/all_gather | solution.py:110
  297.5 8.7 %copy.28 = bf16[12,2048,128]{2,1,0:T(8,128)(2,1)} copy(bf16[12,2048,128]{1,2,0:T(8,128)(2,1)} %all-gather.8.cloned.1.call-done) | data formatting | bytes 12582912 | tf_op jit(solution)/shard_map/all_gather | solution.py:110
  306.2 200.5 %while.21 = (s32[]{:T(128)}, f32[12,128]{1,0:T(8,128)S(1)}, f32[12,128]{1,0:T(8,128)}, f32[12,128]{1,0:T(8,128)}, f32[12,128,128]{2,1,0:T(8,128)S(1)}, /*index=5...) while((s32[]{:T(128)}, f32[12,128]{1,0:T(8,128)S(1)}, ...), condition=%wide.region_4.5_spmd.clone, body=%wide.region_0.4_spmd.clone.sunk | while | flops 306735616 | bytes 14789864 | solution.py:137
  314.2 1.6 convolution_add_fusion.8
  315.8 1.6 convolution_add_fusion.7
  326.8 1.6 convolution_add_fusion.8
  328.3 1.6 convolution_add_fusion.7
  339.3 1.6 convolution_add_fusion.8
  340.9 1.6 convolution_add_fusion.7
  353.5 1.6 convolution_add_fusion.7
  366.1 1.6 convolution_add_fusion.7
  378.6 1.6 convolution_add_fusion.7
  391.2 1.6 convolution_add_fusion.7
  403.8 1.6 convolution_add_fusion.7
  416.3 1.6 convolution_add_fusion.7
  428.9 1.6 convolution_add_fusion.7
  441.5 1.6 convolution_add_fusion.7
  454.1 1.6 convolution_add_fusion.7
  466.7 1.6 convolution_add_fusion.7
  479.2 1.6 convolution_add_fusion.7
  491.8 1.6 convolution_add_fusion.7
  504.4 1.6 convolution_add_fusion.7
  509.2 6.4 %fusion.32 = (f32[3072]{0:T(1024)S(1)}, bf16[1,128,3072]{2,1,0:T(8,128)(2,1)}) fusion(bf16[1,128,3072]{2,1,0:T(8,128)(2,1)} %param.23, f32[3072]{0:T(1024)S(1)} %copy-done.3, bf16[128,1536]{0,1:T(8,128)(2,1)S(1)} %bitcast.115, bf16[1536,3072]{1,0:T(8,128)(2,1)} %param.21), kind=kOutput, calls=%fused_computation.46 | convolution fusion | flops 1209922560 | bytes 11427840 | tf_op jit(solution)/shard_map/dot_general | solution.py:144
  515.5 75.7 %psum.7 = f32[3072]{0:T(1024)S(1)} all-reduce(f32[3072]{0:T(1024)S(1)} %get-tuple-element.187), channel_id=1, replica_groups=mesh['ctx'=16,'dp'=16] {'ctx','dp'}, use_global_device_ids=true, to_apply=%region_6.7 | all-reduce | flops 3072 | bytes 24576 | tf_op jit(solution)/shard_map/psum | solution.py:147
  (297 shorter events, 186.3 us)
Async XLA Ops:
  7.2 139.6 %all-gather.4.cloned.1.call-start = ((), (), s32[]{:S(2)}) async-start(), calls=%async_computation.1 | async-start | bytes 6684672 | tf_op jit(solution)/shard_map/all_gather | solution.py:109
  11.7 5.9 copy-start.2
  16.6 205.1 %all-gather.6.cloned.1.call-start = ((), (), s32[]{:S(2)}) async-start(), calls=%async_computation.2 | async-start | bytes 6684672 | tf_op jit(solution)/shard_map/all_gather | solution.py:111
  17.5 280.0 %all-gather.8.cloned.1.call-start = ((), (), s32[]{:S(2)}) async-start(), calls=%async_computation.3 | async-start | bytes 6684672 | tf_op jit(solution)/shard_map/all_gather | solution.py:110
  24.3 281.9 %all-to-all-start = ((bf16[16,12,128,128]{3,2,1,0:T(8,128)(2,1)}), bf16[16,12,128,128]{3,2,1,0:T(8,128)(2,1)}, u32[]{:S(2)}, u32[]{:S(2)}) async-start(bf16[16,12,128,128]{3,2,1,0:T(8,128)(2,1)} %stack.2), calls=%async_computation | async-start | bytes 12582912 | tf_op jit(solution)/shard_map/all_to_all | solution.py:114
  309.1 8.4 %copy-start = (f32[12,128]{1,0:T(8,128)S(1)}, f32[12,128]{1,0:T(8,128)}, u32[]{:S(2)}) copy-start(f32[12,128]{1,0:T(8,128)} %get-tuple-element.331) | copy-start | bytes 18436 | tf_op jit(solution)/shard_map/while
  320.9 9.1 %copy-start = (f32[12,128]{1,0:T(8,128)S(1)}, f32[12,128]{1,0:T(8,128)}, u32[]{:S(2)}) copy-start(f32[12,128]{1,0:T(8,128)} %get-tuple-element.331) | copy-start | bytes 18436 | tf_op jit(solution)/shard_map/while
  333.5 9.1 %copy-start = (f32[12,128]{1,0:T(8,128)S(1)}, f32[12,128]{1,0:T(8,128)}, u32[]{:S(2)}) copy-start(f32[12,128]{1,0:T(8,128)} %get-tuple-element.331) | copy-start | bytes 18436 | tf_op jit(solution)/shard_map/while
  342.6 0.6 copy-start.1
  346.1 9.1 %copy-start = (f32[12,128]{1,0:T(8,128)S(1)}, f32[12,128]{1,0:T(8,128)}, u32[]{:S(2)}) copy-start(f32[12,128]{1,0:T(8,128)} %get-tuple-element.331) | copy-start | bytes 18436 | tf_op jit(solution)/shard_map/while
  355.2 0.6 copy-start.1
  358.7 9.1 %copy-start = (f32[12,128]{1,0:T(8,128)S(1)}, f32[12,128]{1,0:T(8,128)}, u32[]{:S(2)}) copy-start(f32[12,128]{1,0:T(8,128)} %get-tuple-element.331) | copy-start | bytes 18436 | tf_op jit(solution)/shard_map/while
  367.8 0.6 copy-start.1
  371.2 9.1 %copy-start = (f32[12,128]{1,0:T(8,128)S(1)}, f32[12,128]{1,0:T(8,128)}, u32[]{:S(2)}) copy-start(f32[12,128]{1,0:T(8,128)} %get-tuple-element.331) | copy-start | bytes 18436 | tf_op jit(solution)/shard_map/while
  380.4 0.6 copy-start.1
  383.8 9.1 %copy-start = (f32[12,128]{1,0:T(8,128)S(1)}, f32[12,128]{1,0:T(8,128)}, u32[]{:S(2)}) copy-start(f32[12,128]{1,0:T(8,128)} %get-tuple-element.331) | copy-start | bytes 18436 | tf_op jit(solution)/shard_map/while
  396.4 9.1 %copy-start = (f32[12,128]{1,0:T(8,128)S(1)}, f32[12,128]{1,0:T(8,128)}, u32[]{:S(2)}) copy-start(f32[12,128]{1,0:T(8,128)} %get-tuple-element.331) | copy-start | bytes 18436 | tf_op jit(solution)/shard_map/while
  405.5 0.6 copy-start.1
  409.0 9.1 %copy-start = (f32[12,128]{1,0:T(8,128)S(1)}, f32[12,128]{1,0:T(8,128)}, u32[]{:S(2)}) copy-start(f32[12,128]{1,0:T(8,128)} %get-tuple-element.331) | copy-start | bytes 18436 | tf_op jit(solution)/shard_map/while
  418.1 0.6 copy-start.1
  421.5 9.1 %copy-start = (f32[12,128]{1,0:T(8,128)S(1)}, f32[12,128]{1,0:T(8,128)}, u32[]{:S(2)}) copy-start(f32[12,128]{1,0:T(8,128)} %get-tuple-element.331) | copy-start | bytes 18436 | tf_op jit(solution)/shard_map/while
  430.7 0.6 copy-start.1
  434.1 9.1 %copy-start = (f32[12,128]{1,0:T(8,128)S(1)}, f32[12,128]{1,0:T(8,128)}, u32[]{:S(2)}) copy-start(f32[12,128]{1,0:T(8,128)} %get-tuple-element.331) | copy-start | bytes 18436 | tf_op jit(solution)/shard_map/while
  443.2 0.6 copy-start.1
  446.7 9.1 %copy-start = (f32[12,128]{1,0:T(8,128)S(1)}, f32[12,128]{1,0:T(8,128)}, u32[]{:S(2)}) copy-start(f32[12,128]{1,0:T(8,128)} %get-tuple-element.331) | copy-start | bytes 18436 | tf_op jit(solution)/shard_map/while
  455.8 0.6 copy-start.1
  459.3 9.1 %copy-start = (f32[12,128]{1,0:T(8,128)S(1)}, f32[12,128]{1,0:T(8,128)}, u32[]{:S(2)}) copy-start(f32[12,128]{1,0:T(8,128)} %get-tuple-element.331) | copy-start | bytes 18436 | tf_op jit(solution)/shard_map/while
  468.4 0.6 copy-start.1
  471.9 9.1 %copy-start = (f32[12,128]{1,0:T(8,128)S(1)}, f32[12,128]{1,0:T(8,128)}, u32[]{:S(2)}) copy-start(f32[12,128]{1,0:T(8,128)} %get-tuple-element.331) | copy-start | bytes 18436 | tf_op jit(solution)/shard_map/while
  484.4 9.1 %copy-start = (f32[12,128]{1,0:T(8,128)S(1)}, f32[12,128]{1,0:T(8,128)}, u32[]{:S(2)}) copy-start(f32[12,128]{1,0:T(8,128)} %get-tuple-element.331) | copy-start | bytes 18436 | tf_op jit(solution)/shard_map/while
  497.0 9.1 %copy-start = (f32[12,128]{1,0:T(8,128)S(1)}, f32[12,128]{1,0:T(8,128)}, u32[]{:S(2)}) copy-start(f32[12,128]{1,0:T(8,128)} %get-tuple-element.331) | copy-start | bytes 18436 | tf_op jit(solution)/shard_map/while
  506.7 2.5 copy-start.3
  (6 other events, 3.6 us)
Sparse Core Ops, SparseCore 0:
  16.7 129.9 all-gather.3
  149.3 72.3 all-gather.5
  224.3 73.1 all-gather.7
